TPU v7x, 32 devices: a whole 2x2x4 slice. The times are simulated.
32 devices in a mesh: snap: 2 (over y), row: 4 (over z), col: 4 (over x, core).
Axes of the slice: x: 2, y: 2, z: 4, core: 2. Of those that a mesh axis runs over, the one named last changes fastest.
Arguments:
- orbitals: float32 [12288, 768], P(('snap', 'row', 'col')), parts along dimension 0, may hold values from -6 to 6
- screened: float32 [6, 6144, 6144], P('snap', 'row', 'col'), parts along dimension 0, may hold values from -0.0029296875 to 0.0029296875
- green_weight: float32 [6, 768], P('snap'), parts along dimension 0, may hold values from 0.05 to 1
- time_weight: float32 [3], replicated, may hold values from 0.3 to 1
Outputs:
- updated: float32 [12288, 768], P(('snap', 'row', 'col')), parts along dimension 0
There are 2 independent parts, one for each index of `snap`. A program takes and returns all parts, laid end to end along the dimension named above; an argument that names none is the same for every part. Nothing has to cross between parts.
All inputs are finite; a program needn't handle non-finite values.
Results may differ from a plain program's by a relative error of at most 0.00013.
Values sent between devices are 32-bit elements; how exact they have to be, the bound alone decides.
A program may use at most 128 MiB of HBM per device.

v0:
```python
import jax
import jax.numpy as jnp
from jax import lax
from jax.sharding import PartitionSpec as P

TIMES = 3
PASSES = 2


def from_root(block, axis, owner):
    block = jnp.where(lax.axis_index(axis) == owner, block, jnp.zeros_like(block))
    return lax.psum(block, axis)


def gather_rows(shard):
    return lax.all_gather(shard, "col", axis=0, tiled=True)


def scatter_rows(partial_value):
    return lax.psum_scatter(partial_value, "col", scatter_dimension=0, tiled=True)


def body(orbitals, screened, green_weight, time_weight):
    n_row = lax.axis_size("row")
    n_col = lax.axis_size("col")
    factor = n_col // n_row
    col_width = screened.shape[2]
    col_index = lax.axis_index("col")
    root = col_index // factor
    offset = col_index % factor * col_width
    own = orbitals
    rows = gather_rows(own)
    for step in range(PASSES):
        piece = lax.dynamic_slice_in_dim(rows, offset, col_width, 0)
        columns = from_root(piece, "row", root)
        partial_value = jnp.zeros(rows.shape, jnp.float32)
        for t in range(TIMES):
            green = lax.dot_general(
                rows * green_weight[t],
                columns,
                (((1,), (1,)), ((), ())),
                precision=lax.Precision.HIGHEST,
                preferred_element_type=jnp.float32,
            )
            applied = jnp.dot(
                green * screened[t],
                columns,
                precision=lax.Precision.HIGHEST,
                preferred_element_type=jnp.float32,
            )
            partial_value = partial_value + time_weight[t] * applied
        final = step == PASSES - 1
        own = own - scatter_rows(partial_value)
        if not final:
            rows = gather_rows(own)
    return own


def solution(mesh):
    in_specs = (P(("snap", "row", "col"), None), P("snap", "row", "col"), P("snap", None), P())
    out_specs = P(("snap", "row", "col"), None)
    return jax.shard_map(body, mesh=mesh, in_specs=in_specs, out_specs=out_specs, check_vma=False)
```

profile of v0, /device:TPU:0, one launch (start us, length us, event | category | flops | bytes accessed | tf_op | source)
XLA Modules:
  0.0 877.8 jit_solution(2341078948588468849)
XLA Ops:
  6.5 0.7 all-gather.3.cloned.1.call-update
  7.3 41.8 %all-gather.3.cloned.1.call-done = f32[1536,768]{1,0:T(8,128)} async-done(((f32[384,768]{1,0:T(8,128)}), f32[1536,768]{1,0:T(8,128)}) %all-gather.3.cloned.1.call-update) | async-done | bytes 4718608 | tf_op jit(solution)/shard_map/all_gather | solution.py:16
  49.1 4.8 broadcast_select_fusion.1
  54.5 0.6 fusion.12
  55.2 170.7 %all-reduce.3.cloned.1.call-done = f32[1536,768]{1,0:T(8,128)} async-done(((f32[1536,768]{1,0:T(8,128)}), f32[1536,768]{1,0:T(8,128)}) %all-reduce.3.cloned.1.call-update) | async-done | bytes 4718608 | tf_op jit(solution)/shard_map/psum | solution.py:12
  225.9 28.3 %convolution_multiply_fusion.4 = f32[1536,1536]{1,0:T(8,128)} fusion(f32[1536,768]{1,0:T(8,128)} %all-reduce.3.cloned.1.call-done, f32[3,1536,1536]{2,1,0:T(8,128)} %param.5, f32[1536,768]{1,0:T(8,128)} %all-gather.3.cloned.1.call-done, f32[768]{0:T(1024)S(1)} %get-tuple-element.7), kind=kOutput, calls=%fused_computation.4 | convolution fusion | flops 21746810880 | bytes 28314624 | tf_op jit(solution)/shard_map/dot_general | solution.py:38
  254.2 28.0 %fusion.14 = f32[1536,768]{1,0:T(8,128)} fusion(f32[1536,1536]{1,0:T(8,128)} %convolution_multiply_fusion.4, f32[1536,768]{1,0:T(8,128)} %all-reduce.3.cloned.1.call-done), kind=kOutput, calls=%fused_computation.27 | convolution fusion | flops 21743271936 | bytes 18874368 | tf_op jit(solution)/shard_map/dot_general | solution.py:45
  282.2 26.8 %convolution_multiply_fusion.5 = f32[1536,1536]{1,0:T(8,128)} fusion(f32[1536,768]{1,0:T(8,128)} %all-reduce.3.cloned.1.call-done, f32[3,1536,1536]{2,1,0:T(8,128)S(1)} %bitcast.31, f32[1536,768]{1,0:T(8,128)S(1)} %bitcast.33, f32[768]{0:T(1024)S(1)} %get-tuple-element.6), kind=kOutput, calls=%fused_computation.5 | convolution fusion | flops 21746810880 | bytes 28314624 | tf_op jit(solution)/shard_map/dot_general | solution.py:38
  309.0 27.7 %fusion.13 = f32[1536,768]{1,0:T(8,128)} fusion(f32[1536,1536]{1,0:T(8,128)} %convolution_multiply_fusion.5, f32[1536,768]{1,0:T(8,128)} %all-reduce.3.cloned.1.call-done), kind=kOutput, calls=%fused_computation.26 | convolution fusion | flops 21743271936 | bytes 18874368 | tf_op jit(solution)/shard_map/dot_general | solution.py:45
  336.8 27.0 %convolution_multiply_fusion.3 = f32[1536,1536]{1,0:T(8,128)} fusion(f32[1536,768]{1,0:T(8,128)} %all-reduce.3.cloned.1.call-done, f32[3,1536,1536]{2,1,0:T(8,128)S(1)} %bitcast.31, f32[1536,768]{1,0:T(8,128)S(1)} %bitcast.33, f32[768]{0:T(1024)S(1)} %get-tuple-element.5), kind=kOutput, calls=%fused_computation.3 | convolution fusion | flops 21746810880 | bytes 28314624 | tf_op jit(solution)/shard_map/dot_general | solution.py:38
  363.8 31.6 %multiply_add_fusion.1 = f32[1536,768]{1,0:T(8,128)} fusion(f32[1536,768]{1,0:T(8,128)} %fusion.14, f32[1536,768]{1,0:T(8,128)} %fusion.13, f32[1536,1536]{1,0:T(8,128)} %convolution_multiply_fusion.3, f32[1536,768]{1,0:T(8,128)} %all-reduce.3.cloned.1.call-done, f32[]{:T(128)} %bitcast.4, f32[]{:T(128)} %bitcast.2, f32[]{:T(128)} %bitcast), kind=kOutput, calls=%fused_computation.10 | convolution fusion | flops 21749170176 | bytes 28311564 | tf_op jit(solution)/shard_map/dot_general | solution.py:45
  395.5 47.0 %reduce-scatter.3.cloned.1.call-done = f32[384,768]{1,0:T(8,128)} async-done(((f32[1536,768]{1,0:T(8,128)}), f32[384,768]{1,0:T(8,128)}) %reduce-scatter.3.cloned.1.call-update) | async-done | bytes 1179664 | tf_op jit(solution)/shard_map/reduce_scatter | solution.py:20
  442.5 2.4 sub.8
  445.0 37.5 %all-gather.5.cloned.1.call-done = f32[1536,768]{1,0:T(8,128)} async-done(((f32[384,768]{1,0:T(8,128)}), f32[1536,768]{1,0:T(8,128)}) %all-gather.5.cloned.1.call-update) | async-done | bytes 4718608 | tf_op jit(solution)/shard_map/all_gather | solution.py:16
  482.5 4.8 broadcast_select_fusion
  487.5 171.9 %all-reduce.5.cloned.1.call-done = f32[1536,768]{1,0:T(8,128)} async-done(((f32[1536,768]{1,0:T(8,128)}), f32[1536,768]{1,0:T(8,128)}) %all-reduce.5.cloned.1.call-update) | async-done | bytes 4718608 | tf_op jit(solution)/shard_map/psum | solution.py:12
  659.4 27.4 %convolution_multiply_fusion.1 = f32[1536,1536]{1,0:T(8,128)S(1)} fusion(f32[1536,768]{1,0:T(8,128)} %all-reduce.5.cloned.1.call-done, f32[3,1536,1536]{2,1,0:T(8,128)} %param.5, f32[1536,768]{1,0:T(8,128)} %all-gather.5.cloned.1.call-done, f32[768]{0:T(1024)S(1)} %get-tuple-element.7), kind=kOutput, calls=%fused_computation.1 | convolution fusion | flops 21746810880 | bytes 28314624 | tf_op jit(solution)/shard_map/dot_general | solution.py:38
  686.8 27.3 %convolution_multiply_fusion.2 = f32[1536,1536]{1,0:T(8,128)} fusion(f32[1536,768]{1,0:T(8,128)S(1)} %copy-done, f32[3,1536,1536]{2,1,0:T(8,128)} %param.5, f32[1536,768]{1,0:T(8,128)} %all-gather.5.cloned.1.call-done, f32[768]{0:T(1024)S(1)} %get-tuple-element.6), kind=kOutput, calls=%fused_computation.2 | convolution fusion | flops 21746810880 | bytes 28314624 | tf_op jit(solution)/shard_map/dot_general | solution.py:38
  714.2 28.4 %convolution_multiply_fusion = f32[1536,1536]{1,0:T(8,128)S(1)} fusion(f32[1536,768]{1,0:T(8,128)S(1)} %copy-done, f32[3,1536,1536]{2,1,0:T(8,128)} %param.5, f32[1536,768]{1,0:T(8,128)S(1)} %bitcast.35, f32[768]{0:T(1024)S(1)} %get-tuple-element.5), kind=kOutput, calls=%fused_computation | convolution fusion | flops 21746810880 | bytes 28314624 | tf_op jit(solution)/shard_map/dot_general | solution.py:38
  742.6 23.3 %fusion.16 = f32[1536,768]{1,0:T(8,128)S(1)} fusion(f32[1536,1536]{1,0:T(8,128)S(1)} %convolution_multiply_fusion.1, f32[1536,768]{1,0:T(8,128)S(1)} %copy-done), kind=kOutput, calls=%fused_computation.29 | convolution fusion | flops 21743271936 | bytes 18874368 | tf_op jit(solution)/shard_map/dot_general | solution.py:45
  765.9 28.4 %fusion.15 = f32[1536,768]{1,0:T(8,128)S(1)} fusion(f32[1536,1536]{1,0:T(8,128)} %convolution_multiply_fusion.2, f32[1536,768]{1,0:T(8,128)S(1)} %copy-done), kind=kOutput, calls=%fused_computation.28 | convolution fusion | flops 21743271936 | bytes 18874368 | tf_op jit(solution)/shard_map/dot_general | solution.py:45
  794.2 27.0 %multiply_add_fusion = f32[1536,768]{1,0:T(8,128)} fusion(f32[1536,768]{1,0:T(8,128)S(1)} %fusion.16, f32[1536,768]{1,0:T(8,128)S(1)} %fusion.15, f32[1536,1536]{1,0:T(8,128)S(1)} %convolution_multiply_fusion, f32[1536,768]{1,0:T(8,128)S(1)} %copy-done, f32[]{:T(128)} %bitcast.4, f32[]{:T(128)} %bitcast.2, f32[]{:T(128)} %bitcast), kind=kOutput, calls=%fused_computation.6 | convolution fusion | flops 21749170176 | bytes 28311564 | tf_op jit(solution)/shard_map/dot_general | solution.py:45
  821.2 47.1 %reduce-scatter.5.cloned.1.call-done = f32[384,768]{1,0:T(8,128)} async-done(((f32[1536,768]{1,0:T(8,128)}), f32[384,768]{1,0:T(8,128)}) %reduce-scatter.5.cloned.1.call-update) | async-done | bytes 1179664 | tf_op jit(solution)/shard_map/reduce_scatter | solution.py:20
  868.3 2.4 sub.9
  (47 shorter events, 1.0 us)
Async XLA Ops:
  6.5 42.5 %all-gather.3.cloned.1.call-start = ((), (), s32[]{:S(2)}) async-start(), calls=%async_computation.2 | async-start | bytes 5898240 | tf_op jit(solution)/shard_map/all_gather | solution.py:16
  7.3 218.6 %all-reduce.3.cloned.1.call-start = ((), (), s32[]{:S(2)}) async-start(), calls=%async_computation.3 | async-start | bytes 9437184 | tf_op jit(solution)/shard_map/psum | solution.py:12
  53.9 0.7 copy-start.4
  53.9 1.3 copy-start.3
  53.9 228.3 %slice-start.7 = ((s8[4718592]{0:T(1024)(128)(4,1)}), s8[524288]{0:T(1024)(128)(4,1)S(1)}, s32[]{:S(2)}) async-start(s8[4718592]{0:T(1024)(128)(4,1)} %bitcast.32), calls=%async_computation.15 | async-start | bytes 1048576
  53.9 388.6 %reduce-scatter.3.cloned.1.call-start = ((), (), s32[]{:S(2)}) async-start(), calls=%async_computation.4 | async-start | bytes 5898240 | tf_op jit(solution)/shard_map/reduce_scatter | solution.py:20
  225.9 56.3 %slice-start = ((s8[28311552]{0:T(1024)(128)(4,1)}), s8[4194304]{0:T(1024)(128)(4,1)S(1)}, s32[]{:S(2)}) async-start(s8[28311552]{0:T(1024)(128)(4,1)} %bitcast.30), calls=%async_computation.8 | async-start | bytes 8388608
  225.9 56.3 %slice-start.1 = ((s8[28311552]{0:T(1024)(128)(4,1)}), s8[4194304]{0:T(1024)(128)(4,1)S(1)}, s32[]{:S(2)}) async-start(s8[28311552]{0:T(1024)(128)(4,1)} %bitcast.30), calls=%async_computation.9 | async-start | bytes 8388608
  225.9 56.3 %slice-start.2 = ((s8[28311552]{0:T(1024)(128)(4,1)}), s8[4194304]{0:T(1024)(128)(4,1)S(1)}, s32[]{:S(2)}) async-start(s8[28311552]{0:T(1024)(128)(4,1)} %bitcast.30), calls=%async_computation.10 | async-start | bytes 8388608
  225.9 56.3 %slice-start.3 = ((s8[28311552]{0:T(1024)(128)(4,1)}), s8[4194304]{0:T(1024)(128)(4,1)S(1)}, s32[]{:S(2)}) async-start(s8[28311552]{0:T(1024)(128)(4,1)} %bitcast.30), calls=%async_computation.11 | async-start | bytes 8388608
  225.9 56.3 %slice-start.8 = ((s8[4718592]{0:T(1024)(128)(4,1)}), s8[4194304]{0:T(1024)(128)(4,1)S(1)}, s32[]{:S(2)}) async-start(s8[4718592]{0:T(1024)(128)(4,1)} %bitcast.32), calls=%async_computation.16 | async-start | bytes 8388608
  254.1 28.0 %slice-start.4 = ((s8[28311552]{0:T(1024)(128)(4,1)}), s8[4194304]{0:T(1024)(128)(4,1)S(1)}, s32[]{:S(2)}) async-start(s8[28311552]{0:T(1024)(128)(4,1)} %bitcast.30), calls=%async_computation.12 | async-start | bytes 8388608
  254.1 28.1 %slice-start.5 = ((s8[28311552]{0:T(1024)(128)(4,1)}), s8[4194304]{0:T(1024)(128)(4,1)S(1)}, s32[]{:S(2)}) async-start(s8[28311552]{0:T(1024)(128)(4,1)} %bitcast.30), calls=%async_computation.13 | async-start | bytes 8388608
  254.2 28.1 %slice-start.6 = ((s8[28311552]{0:T(1024)(128)(4,1)}), s8[3145728]{0:T(1024)(128)(4,1)S(1)}, s32[]{:S(2)}) async-start(s8[28311552]{0:T(1024)(128)(4,1)} %bitcast.30), calls=%async_computation.14 | async-start | bytes 6291456
  395.4 47.1 %copy-start.2 = (f32[384,768]{1,0:T(8,128)S(1)}, f32[384,768]{1,0:T(8,128)}, u32[]{:S(2)}) copy-start(f32[384,768]{1,0:T(8,128)} %param.4) | copy-start | bytes 3538948
  395.4 87.1 %all-gather.5.cloned.1.call-start = ((), (), s32[]{:S(2)}) async-start(), calls=%async_computation.5 | async-start | bytes 5898240 | tf_op jit(solution)/shard_map/all_gather | solution.py:16
  445.0 214.4 %all-reduce.5.cloned.1.call-start = ((), (), s32[]{:S(2)}) async-start(), calls=%async_computation.6 | async-start | bytes 9437184 | tf_op jit(solution)/shard_map/psum | solution.py:12
  487.4 380.9 %reduce-scatter.5.cloned.1.call-start = ((), (), s32[]{:S(2)}) async-start(), calls=%async_computation.7 | async-start | bytes 5898240 | tf_op jit(solution)/shard_map/reduce_scatter | solution.py:20
  659.4 27.4 %copy-start = (f32[1536,768]{1,0:T(8,128)S(1)}, f32[1536,768]{1,0:T(8,128)}, u32[]{:S(2)}) copy-start(f32[1536,768]{1,0:T(8,128)} %all-reduce.5.cloned.1.call-done) | copy-start | bytes 14155780
  659.4 54.8 %slice-start.9 = ((s8[4718592]{0:T(1024)(128)(4,1)}), s8[4194304]{0:T(1024)(128)(4,1)S(1)}, s32[]{:S(2)}) async-start(s8[4718592]{0:T(1024)(128)(4,1)} %bitcast.34), calls=%async_computation.17 | async-start | bytes 8388608
  686.8 27.3 %slice-start.10 = ((s8[4718592]{0:T(1024)(128)(4,1)}), s8[524288]{0:T(1024)(128)(4,1)S(1)}, s32[]{:S(2)}) async-start(s8[4718592]{0:T(1024)(128)(4,1)} %bitcast.34), calls=%async_computation.18 | async-start | bytes 1048576
  821.2 47.1 %copy-start.1 = (f32[384,768]{1,0:T(8,128)S(1)}, f32[384,768]{1,0:T(8,128)}, u32[]{:S(2)}) copy-start(f32[384,768]{1,0:T(8,128)} %sub.8) | copy-start | bytes 3538948
Sparse Core Ops, SparseCore 0:
  8.9 40.1 all-gather.2
  54.0 171.8 all-reduce.2
  395.5 46.9 reduce-scatter.2
  445.1 37.4 all-gather.4
  487.5 171.8 all-reduce.4
  821.4 46.9 reduce-scatter.4
where the time goes:
time: 886 us; the launch traced here: 878 us
  waiting for transfers between devices  517 us (58%)
  matrix products  331 us (37%)
  other arithmetic  14.5 us (2%)
  between operations  13.9 us (2%)
    psum x2, waiting for transfers between devices, from_root(): return lax.psum(block, axis)  343 us
    dot_general x6, matrix products, body(): jnp.dot(green * screened[t], columns, precision=lax.Precision.HIGHEST, pr...  166 us
    dot_general x6, matrix products, body(): lax.dot_general(rows * green_weight[t], columns, (((1,), (1,)), ((), ()))...  165 us
    reduce_scatter x2, waiting for transfers between devices, scatter_rows(): lax.psum_scatter(partial_value, 'col', scatter_dimension=0, tiled=True)  94.1 us
    all_gather x2, waiting for transfers between devices, gather_rows(): return lax.all_gather(shard, 'col', axis=0, tiled=True)  79.3 us
  transfers between devices with their start and end apart: 6, of which 6 were waited for; matrix products, arithmetic and copies ran while one was open for 0% of the time, Pallas kernels for 0%

commit v1 on v0

--- a/solution.py
+++ b/solution.py
@@ -9,7 +9,8 @@
 
 def from_root(block, axis, owner):
     block = jnp.where(lax.axis_index(axis) == owner, block, jnp.zeros_like(block))
-    return lax.psum(block, axis)
+    link_halves_here = lambda tile_in, axis_key: jnp.sum(lax.all_gather(tile_in, axis_key), 0)
+    return link_halves_here(block, axis)
 
 
 def gather_rows(shard):

time: 886 us -> 1210 us (1.37)
  waiting for transfers between devices: 517 us -> 818 us
  other arithmetic: 14.5 us -> 35.2 us
    all_gather x0 -> x2, waiting for transfers between devices: none -> 644 us  [from_root(): lax.all_gather(tile_in, axis_key)]
    psum x2 -> x0, waiting for transfers between devices: 343 us -> none  [from_root(): return lax.psum(block, axis)]
    reduce_sum x0 -> x2, other arithmetic: none -> 20.8 us  [from_root(): jnp.sum(lax.all_gather(tile_in, axis_key), 0)]
where the time goes in v1:
time: 1210 us
  waiting for transfers between devices  818 us (68%)
  matrix products  339 us (28%)
  other arithmetic  35.2 us (3%)
  between operations  13.9 us (1%)
    all_gather x2, waiting for transfers between devices, from_root(): lax.all_gather(tile_in, axis_key)  644 us
    dot_general x6, matrix products, body(): jnp.dot(green * screened[t], columns, precision=lax.Precision.HIGHEST, pr...  175 us
    dot_general x6, matrix products, body(): lax.dot_general(rows * green_weight[t], columns, (((1,), (1,)), ((), ()))...  164 us
    reduce_scatter x2, waiting for transfers between devices, scatter_rows(): lax.psum_scatter(partial_value, 'col', scatter_dimension=0, tiled=True)  93.9 us
    all_gather x2, waiting for transfers between devices, gather_rows(): return lax.all_gather(shard, 'col', axis=0, tiled=True)  79.3 us
  transfers between devices with their start and end apart: 6, of which 6 were waited for; matrix products, arithmetic and copies ran while one was open for 0% of the time, Pallas kernels for 0%

profile of v1, /device:TPU:0, one launch (start us, length us, event | category | flops | bytes accessed | tf_op | source)
XLA Modules:
  0.0 1207.3 jit_solution(12461725232774533941)
XLA Ops:
  7.3 41.8 %all-gather.7.cloned.1.call-done = f32[1536,768]{1,0:T(8,128)} async-done(((f32[384,768]{1,0:T(8,128)}), f32[1536,768]{1,0:T(8,128)}) %all-gather.7.cloned.1.call-update) | async-done | bytes 4718608 | tf_op jit(solution)/shard_map/all_gather | solution.py:17
  49.1 4.8 broadcast_select_fusion.1
  55.3 321.3 %all-gather.11.cloned.1.call-done = f32[6144,768]{1,0:T(8,128)} async-done(((f32[1536,768]{1,0:T(8,128)}), f32[6144,768]{1,0:T(8,128)}) %all-gather.11.cloned.1.call-update) | async-done | bytes 18874384 | tf_op jit(solution)/shard_map/all_gather | solution.py:12
  376.5 10.4 reduce_sum.18
  386.9 28.4 %convolution_multiply_fusion.4 = f32[1536,1536]{1,0:T(8,128)} fusion(f32[1536,768]{1,0:T(8,128)} %reduce_sum.18, f32[3,1536,1536]{2,1,0:T(8,128)} %param.5, f32[1536,768]{1,0:T(8,128)} %all-gather.7.cloned.1.call-done, f32[768]{0:T(1024)S(1)} %get-tuple-element.7), kind=kOutput, calls=%fused_computation.4 | convolution fusion | flops 21746810880 | bytes 28314624 | tf_op jit(solution)/shard_map/dot_general | solution.py:39
  415.4 28.0 %fusion.14 = f32[1536,768]{1,0:T(8,128)} fusion(f32[1536,1536]{1,0:T(8,128)} %convolution_multiply_fusion.4, f32[1536,768]{1,0:T(8,128)} %reduce_sum.18), kind=kOutput, calls=%fused_computation.27 | convolution fusion | flops 21743271936 | bytes 18874368 | tf_op jit(solution)/shard_map/dot_general | solution.py:46
  443.5 26.8 %convolution_multiply_fusion.5 = f32[1536,1536]{1,0:T(8,128)} fusion(f32[1536,768]{1,0:T(8,128)} %reduce_sum.18, f32[3,1536,1536]{2,1,0:T(8,128)S(1)} %bitcast.33, f32[1536,768]{1,0:T(8,128)S(1)} %bitcast.37, f32[768]{0:T(1024)S(1)} %get-tuple-element.6), kind=kOutput, calls=%fused_computation.5 | convolution fusion | flops 21746810880 | bytes 28314624 | tf_op jit(solution)/shard_map/dot_general | solution.py:39
  470.3 27.8 %fusion.13 = f32[1536,768]{1,0:T(8,128)} fusion(f32[1536,1536]{1,0:T(8,128)} %convolution_multiply_fusion.5, f32[1536,768]{1,0:T(8,128)} %reduce_sum.18), kind=kOutput, calls=%fused_computation.26 | convolution fusion | flops 21743271936 | bytes 18874368 | tf_op jit(solution)/shard_map/dot_general | solution.py:46
  498.0 27.0 %convolution_multiply_fusion.3 = f32[1536,1536]{1,0:T(8,128)} fusion(f32[1536,768]{1,0:T(8,128)} %reduce_sum.18, f32[3,1536,1536]{2,1,0:T(8,128)S(1)} %bitcast.33, f32[1536,768]{1,0:T(8,128)S(1)} %bitcast.37, f32[768]{0:T(1024)S(1)} %get-tuple-element.5), kind=kOutput, calls=%fused_computation.3 | convolution fusion | flops 21746810880 | bytes 28314624 | tf_op jit(solution)/shard_map/dot_general | solution.py:39
  525.0 31.6 %multiply_add_fusion.1 = f32[1536,768]{1,0:T(8,128)} fusion(f32[1536,768]{1,0:T(8,128)} %fusion.14, f32[1536,768]{1,0:T(8,128)} %fusion.13, f32[1536,1536]{1,0:T(8,128)} %convolution_multiply_fusion.3, f32[1536,768]{1,0:T(8,128)} %reduce_sum.18, f32[]{:T(128)} %bitcast.5, f32[]{:T(128)} %bitcast.3, f32[]{:T(128)} %bitcast), kind=kOutput, calls=%fused_computation.10 | convolution fusion | flops 21749170176 | bytes 28311564 | tf_op jit(solution)/shard_map/dot_general | solution.py:46
  556.8 46.9 %reduce-scatter.3.cloned.1.call-done = f32[384,768]{1,0:T(8,128)} async-done(((f32[1536,768]{1,0:T(8,128)}), f32[384,768]{1,0:T(8,128)}) %reduce-scatter.3.cloned.1.call-update) | async-done | bytes 1179664 | tf_op jit(solution)/shard_map/reduce_scatter | solution.py:21
  603.7 2.4 sub.8
  606.2 37.5 %all-gather.9.cloned.1.call-done = f32[1536,768]{1,0:T(8,128)} async-done(((f32[384,768]{1,0:T(8,128)}), f32[1536,768]{1,0:T(8,128)}) %all-gather.9.cloned.1.call-update) | async-done | bytes 4718608 | tf_op jit(solution)/shard_map/all_gather | solution.py:17
  643.7 4.8 broadcast_select_fusion
  648.6 322.6 %all-gather.13.cloned.1.call-done = f32[6144,768]{1,0:T(8,128)} async-done(((f32[1536,768]{1,0:T(8,128)}), f32[6144,768]{1,0:T(8,128)}) %all-gather.13.cloned.1.call-update) | async-done | bytes 18874384 | tf_op jit(solution)/shard_map/all_gather | solution.py:12
  971.2 10.4 reduce_sum.19
  981.6 28.2 %convolution_multiply_fusion.1 = f32[1536,1536]{1,0:T(8,128)} fusion(f32[1536,768]{1,0:T(8,128)} %reduce_sum.19, f32[3,1536,1536]{2,1,0:T(8,128)} %param.5, f32[1536,768]{1,0:T(8,128)} %all-gather.9.cloned.1.call-done, f32[768]{0:T(1024)S(1)} %get-tuple-element.7), kind=kOutput, calls=%fused_computation.1 | convolution fusion | flops 21746810880 | bytes 28314624 | tf_op jit(solution)/shard_map/dot_general | solution.py:39
  1009.8 27.9 %fusion.16 = f32[1536,768]{1,0:T(8,128)} fusion(f32[1536,1536]{1,0:T(8,128)} %convolution_multiply_fusion.1, f32[1536,768]{1,0:T(8,128)} %reduce_sum.19), kind=kOutput, calls=%fused_computation.29 | convolution fusion | flops 21743271936 | bytes 18874368 | tf_op jit(solution)/shard_map/dot_general | solution.py:46
  1037.8 27.0 %convolution_multiply_fusion.2 = f32[1536,1536]{1,0:T(8,128)} fusion(f32[1536,768]{1,0:T(8,128)} %reduce_sum.19, f32[3,1536,1536]{2,1,0:T(8,128)S(1)} %bitcast.35, f32[1536,768]{1,0:T(8,128)S(1)} %bitcast.39, f32[768]{0:T(1024)S(1)} %get-tuple-element.6), kind=kOutput, calls=%fused_computation.2 | convolution fusion | flops 21746810880 | bytes 28314624 | tf_op jit(solution)/shard_map/dot_general | solution.py:39
  1064.8 27.8 %fusion.15 = f32[1536,768]{1,0:T(8,128)} fusion(f32[1536,1536]{1,0:T(8,128)} %convolution_multiply_fusion.2, f32[1536,768]{1,0:T(8,128)} %reduce_sum.19), kind=kOutput, calls=%fused_computation.28 | convolution fusion | flops 21743271936 | bytes 18874368 | tf_op jit(solution)/shard_map/dot_general | solution.py:46
  1092.7 26.7 %convolution_multiply_fusion = f32[1536,1536]{1,0:T(8,128)} fusion(f32[1536,768]{1,0:T(8,128)} %reduce_sum.19, f32[3,1536,1536]{2,1,0:T(8,128)S(1)} %bitcast.35, f32[1536,768]{1,0:T(8,128)S(1)} %bitcast.39, f32[768]{0:T(1024)S(1)} %get-tuple-element.5), kind=kOutput, calls=%fused_computation | convolution fusion | flops 21746810880 | bytes 28314624 | tf_op jit(solution)/shard_map/dot_general | solution.py:39
  1119.4 31.5 %multiply_add_fusion = f32[1536,768]{1,0:T(8,128)} fusion(f32[1536,768]{1,0:T(8,128)} %fusion.16, f32[1536,768]{1,0:T(8,128)} %fusion.15, f32[1536,1536]{1,0:T(8,128)} %convolution_multiply_fusion, f32[1536,768]{1,0:T(8,128)} %reduce_sum.19, f32[]{:T(128)} %bitcast.5, f32[]{:T(128)} %bitcast.3, f32[]{:T(128)} %bitcast), kind=kOutput, calls=%fused_computation.6 | convolution fusion | flops 21749170176 | bytes 28311564 | tf_op jit(solution)/shard_map/dot_general | solution.py:46
  1150.9 47.0 %reduce-scatter.5.cloned.1.call-done = f32[384,768]{1,0:T(8,128)} async-done(((f32[1536,768]{1,0:T(8,128)}), f32[384,768]{1,0:T(8,128)}) %reduce-scatter.5.cloned.1.call-update) | async-done | bytes 1179664 | tf_op jit(solution)/shard_map/reduce_scatter | solution.py:21
  1197.9 2.4 sub.9
  (62 shorter events, 2.4 us)
Async XLA Ops:
  6.5 42.5 %all-gather.7.cloned.1.call-start = ((), (), s32[]{:S(2)}) async-start(), calls=%async_computation.2 | async-start | bytes 5898240 | tf_op jit(solution)/shard_map/all_gather | solution.py:17
  7.3 369.3 %all-gather.11.cloned.1.call-start = ((), (), s32[]{:S(2)}) async-start(), calls=%async_computation.6 | async-start | bytes 23592960 | tf_op jit(solution)/shard_map/all_gather | solution.py:12
  53.9 549.8 %reduce-scatter.3.cloned.1.call-start = ((), (), s32[]{:S(2)}) async-start(), calls=%async_computation.3 | async-start | bytes 5898240 | tf_op jit(solution)/shard_map/reduce_scatter | solution.py:21
  376.5 66.8 %slice-start.14 = ((s8[4718592]{0:T(1024)(128)(4,1)}), s8[524288]{0:T(1024)(128)(4,1)S(1)}, s32[]{:S(2)}) async-start(s8[4718592]{0:T(1024)(128)(4,1)} %bitcast.36), calls=%async_computation.22 | async-start | bytes 1048576
  386.9 56.4 %slice-start = ((s8[28311552]{0:T(1024)(128)(4,1)}), s8[4194304]{0:T(1024)(128)(4,1)S(1)}, s32[]{:S(2)}) async-start(s8[28311552]{0:T(1024)(128)(4,1)} %bitcast.32), calls=%async_computation.8 | async-start | bytes 8388608
  386.9 56.4 %slice-start.1 = ((s8[28311552]{0:T(1024)(128)(4,1)}), s8[4194304]{0:T(1024)(128)(4,1)S(1)}, s32[]{:S(2)}) async-start(s8[28311552]{0:T(1024)(128)(4,1)} %bitcast.32), calls=%async_computation.9 | async-start | bytes 8388608
  386.9 56.4 %slice-start.2 = ((s8[28311552]{0:T(1024)(128)(4,1)}), s8[4194304]{0:T(1024)(128)(4,1)S(1)}, s32[]{:S(2)}) async-start(s8[28311552]{0:T(1024)(128)(4,1)} %bitcast.32), calls=%async_computation.10 | async-start | bytes 8388608
  386.9 56.5 %slice-start.3 = ((s8[28311552]{0:T(1024)(128)(4,1)}), s8[4194304]{0:T(1024)(128)(4,1)S(1)}, s32[]{:S(2)}) async-start(s8[28311552]{0:T(1024)(128)(4,1)} %bitcast.32), calls=%async_computation.11 | async-start | bytes 8388608
  386.9 56.5 %slice-start.15 = ((s8[4718592]{0:T(1024)(128)(4,1)}), s8[4194304]{0:T(1024)(128)(4,1)S(1)}, s32[]{:S(2)}) async-start(s8[4718592]{0:T(1024)(128)(4,1)} %bitcast.36), calls=%async_computation.23 | async-start | bytes 8388608
  415.3 28.1 %slice-start.4 = ((s8[28311552]{0:T(1024)(128)(4,1)}), s8[4194304]{0:T(1024)(128)(4,1)S(1)}, s32[]{:S(2)}) async-start(s8[28311552]{0:T(1024)(128)(4,1)} %bitcast.32), calls=%async_computation.12 | async-start | bytes 8388608
  415.3 28.1 %slice-start.5 = ((s8[28311552]{0:T(1024)(128)(4,1)}), s8[4194304]{0:T(1024)(128)(4,1)S(1)}, s32[]{:S(2)}) async-start(s8[28311552]{0:T(1024)(128)(4,1)} %bitcast.32), calls=%async_computation.13 | async-start | bytes 8388608
  415.4 28.1 %slice-start.6 = ((s8[28311552]{0:T(1024)(128)(4,1)}), s8[3145728]{0:T(1024)(128)(4,1)S(1)}, s32[]{:S(2)}) async-start(s8[28311552]{0:T(1024)(128)(4,1)} %bitcast.32), calls=%async_computation.14 | async-start | bytes 6291456
  556.7 47.0 %copy-start.1 = (f32[384,768]{1,0:T(8,128)S(1)}, f32[384,768]{1,0:T(8,128)}, u32[]{:S(2)}) copy-start(f32[384,768]{1,0:T(8,128)} %param.4) | copy-start | bytes 3538948
  556.7 87.0 %all-gather.9.cloned.1.call-start = ((), (), s32[]{:S(2)}) async-start(), calls=%async_computation.4 | async-start | bytes 5898240 | tf_op jit(solution)/shard_map/all_gather | solution.py:17
  606.2 365.0 %all-gather.13.cloned.1.call-start = ((), (), s32[]{:S(2)}) async-start(), calls=%async_computation.7 | async-start | bytes 23592960 | tf_op jit(solution)/shard_map/all_gather | solution.py:12
  648.6 549.3 %reduce-scatter.5.cloned.1.call-start = ((), (), s32[]{:S(2)}) async-start(), calls=%async_computation.5 | async-start | bytes 5898240 | tf_op jit(solution)/shard_map/reduce_scatter | solution.py:21
  971.2 66.6 %slice-start.16 = ((s8[4718592]{0:T(1024)(128)(4,1)}), s8[524288]{0:T(1024)(128)(4,1)S(1)}, s32[]{:S(2)}) async-start(s8[4718592]{0:T(1024)(128)(4,1)} %bitcast.38), calls=%async_computation.24 | async-start | bytes 1048576
  981.6 56.2 %slice-start.7 = ((s8[28311552]{0:T(1024)(128)(4,1)}), s8[4194304]{0:T(1024)(128)(4,1)S(1)}, s32[]{:S(2)}) async-start(s8[28311552]{0:T(1024)(128)(4,1)} %bitcast.34), calls=%async_computation.15 | async-start | bytes 8388608
  981.6 56.2 %slice-start.8 = ((s8[28311552]{0:T(1024)(128)(4,1)}), s8[4194304]{0:T(1024)(128)(4,1)S(1)}, s32[]{:S(2)}) async-start(s8[28311552]{0:T(1024)(128)(4,1)} %bitcast.34), calls=%async_computation.16 | async-start | bytes 8388608
  981.6 56.2 %slice-start.9 = ((s8[28311552]{0:T(1024)(128)(4,1)}), s8[4194304]{0:T(1024)(128)(4,1)S(1)}, s32[]{:S(2)}) async-start(s8[28311552]{0:T(1024)(128)(4,1)} %bitcast.34), calls=%async_computation.17 | async-start | bytes 8388608
  981.6 56.2 %slice-start.10 = ((s8[28311552]{0:T(1024)(128)(4,1)}), s8[4194304]{0:T(1024)(128)(4,1)S(1)}, s32[]{:S(2)}) async-start(s8[28311552]{0:T(1024)(128)(4,1)} %bitcast.34), calls=%async_computation.18 | async-start | bytes 8388608
  981.6 56.2 %slice-start.17 = ((s8[4718592]{0:T(1024)(128)(4,1)}), s8[4194304]{0:T(1024)(128)(4,1)S(1)}, s32[]{:S(2)}) async-start(s8[4718592]{0:T(1024)(128)(4,1)} %bitcast.38), calls=%async_computation.25 | async-start | bytes 8388608
  1009.8 28.0 %slice-start.13 = ((s8[28311552]{0:T(1024)(128)(4,1)}), s8[3145728]{0:T(1024)(128)(4,1)S(1)}, s32[]{:S(2)}) async-start(s8[28311552]{0:T(1024)(128)(4,1)} %bitcast.34), calls=%async_computation.21 | async-start | bytes 6291456
  1150.9 47.0 %copy-start = (f32[384,768]{1,0:T(8,128)S(1)}, f32[384,768]{1,0:T(8,128)}, u32[]{:S(2)}) copy-start(f32[384,768]{1,0:T(8,128)} %sub.8) | copy-start | bytes 3538948
  (4 other events, 58.0 us)
Sparse Core Ops, SparseCore 0:
  8.9 40.1 all-gather.6
  54.0 322.4 all-gather.10
  556.9 46.8 reduce-scatter.2
  606.3 37.4 all-gather.8
  648.7 322.4 all-gather.12
  1151.0 46.8 reduce-scatter.4
